TPU v7x, 32 devices: a whole 2x2x4 slice. The times are simulated.
32 devices in a mesh: frames: 4 (over y, x), rows: 8 (over z, core).
Axes of the slice: x: 2, y: 2, z: 4, core: 2. Of those that a mesh axis runs over, the one named last changes fastest.
Arguments:
- inputs: bfloat16 [4, 32, 424, 256], P('frames', 'rows'), may hold values from -350 to 350, as said below
- cotangent: bfloat16 [4, 32, 424, 256], P('frames', 'rows'), may hold values from -140 to 140, as said below
- kernel: bfloat16 [3, 3, 3, 256, 256], replicated, may hold values from -0.078125 to 0.078125
- norm_gain: float32 [256], replicated, may hold values from 0.1 to 1.9
- norm_bias: float32 [256], replicated, may hold values from -1 to 1
Outputs:
- input_grad: bfloat16 [4, 32, 424, 256], P('frames', 'rows')
Inputs may be any that keep to these rules, and one draw needn't show every extreme that they name: `inputs`: finite values. `cotangent`: finite values.
All inputs are finite; a program needn't handle non-finite values.
Results may differ from a plain program's by a relative error of at most 0.0055.
Values may be sent and summed in bfloat16 or wider, within the bound.
No kernel may reach another device: no remote copies, remote signals or barrier semaphores. Data moves between devices by JAX's collectives and lax.ppermute only.
A program may use at most 64 MiB of HBM per device.

v0:
```python
import jax
import jax.numpy as jnp
from jax import lax
from jax.sharding import PartitionSpec as P

GROUPS = 32
EPS = 1e-06


def from_behind(value, axis, by):
    devices = lax.axis_size(axis)
    pairs = [(i, i + by) for i in range(devices) if 0 <= i + by < devices]
    return lax.ppermute(value, axis, pairs)


def padded_2(value, sides, width):
    for axis, dim in sides:
        devices, length = (lax.axis_size(axis), value.shape[dim])
        up = [(i, (i + 1) % devices) for i in range(devices - 1)]
        down = [(j, i) for i, j in up]
        last = lax.slice_in_dim(value, length - width, length, axis=dim)
        first = lax.slice_in_dim(value, 0, width, axis=dim)
        before = lax.ppermute(last, axis, up)
        after = lax.ppermute(first, axis, down)
        value = jnp.concatenate([before, value, after], axis=dim)
    return value


def group_sum(values):
    per_chan = jnp.sum(values, axis=(0, 1))
    return jnp.sum(per_chan.reshape(GROUPS, -1), axis=1)


def spread_groups(per_group, channels):
    return jnp.repeat(per_group, channels // GROUPS)


def transpose_conv(rimmed, flipped, strip, width, channels):
    padded = jnp.pad(rimmed, ((0, 0), (0, 0), (1, 1), (0, 0)))
    act_grad = jnp.zeros((strip, width, channels), jnp.float32)
    for row_tap in range(3):
        for col_tap in range(3):
            window = padded[
                :, 2 - row_tap : 2 - row_tap + strip, 2 - col_tap : 2 - col_tap + width, :
            ]
            act_grad = act_grad + jnp.einsum(
                "myxo,mco->yxc",
                window,
                flipped[:, row_tap, col_tap],
                preferred_element_type=jnp.float32,
            )
    return act_grad


def shards(inputs, cotangent, kernel, norm_gain, norm_bias):
    values = inputs[0].astype(jnp.float32)
    strip, width, channels = values.shape
    cells_per = (
        lax.axis_size("frames") * lax.axis_size("rows") * strip * width * (channels // GROUPS)
    )
    flipped = kernel[::-1]
    own_slab = cotangent[0]
    later = from_behind(own_slab, "frames", -1)
    latest = from_behind(own_slab, "frames", -2)
    stacked = jnp.stack([own_slab, later, latest])
    rimmed = padded_2(stacked, (("rows", 1),), 1)
    act_grad = transpose_conv(rimmed, flipped, strip, width, channels)
    totals, squares = lax.psum((group_sum(values), group_sum(values * values)), ("frames", "rows"))
    centre = totals / cells_per
    variance = jnp.maximum(squares / cells_per - centre * centre, 0.0)
    centred = values - spread_groups(centre, channels)
    inv_std = spread_groups(lax.rsqrt(variance + EPS), channels)
    normed = centred * inv_std
    preact = normed * norm_gain + norm_bias
    logistic = jax.nn.sigmoid(preact)
    norm_grad = act_grad * logistic * (1.0 + preact * (1.0 - logistic)) * norm_gain
    grad_total, grad_cross = lax.psum(
        (group_sum(norm_grad), group_sum(norm_grad * normed)), ("frames", "rows")
    )
    grad_total = grad_total / cells_per
    grad_cross = grad_cross / cells_per
    input_grad = inv_std * (
        norm_grad
        - spread_groups(grad_total, channels)
        - normed * spread_groups(grad_cross, channels)
    )
    return input_grad.astype(jnp.bfloat16)[None]


def solution(mesh):
    return jax.shard_map(
        shards,
        mesh=mesh,
        in_specs=(P("frames", "rows", None, None), P("frames", "rows", None, None), P(), P(), P()),
        out_specs=P("frames", "rows", None, None),
        check_vma=False,
    )
```

profile of v0, /device:TPU:14, one launch (start us, length us, event | category | flops | bytes accessed | tf_op | source)
XLA Modules:
  0.0 156.6 jit_solution(9935320973470033081)
XLA Ops:
  0.0 3.3 %collective-permute-start.1 = (bf16[4,424,256]{2,1,0:T(8,128)(2,1)}, bf16[4,424,256]{2,1,0:T(8,128)(2,1)}, u32[]{:S(2)}, u32[]{:S(2)}) collective-permute-start(bf16[4,424,256]{2,1,0:T(8,128)(2,1)} %bitcast.146), channel_id=1, source_target_pairs={{16,0},{24,8},{17,1},{25,9},{18,2},{26,10},{19,3},{27,11},{20,4},{... | collective-permute-start | bytes 2605064 | tf_op jit(solution)/shard_map/ppermute | solution.py:13
  3.3 3.4 %collective-permute-start = (bf16[4,424,256]{2,1,0:T(8,128)(2,1)}, bf16[4,424,256]{2,1,0:T(8,128)(2,1)}, u32[]{:S(2)}, u32[]{:S(2)}) collective-permute-start(bf16[4,424,256]{2,1,0:T(8,128)(2,1)} %bitcast.147), channel_id=1, source_target_pairs={{8,0},{16,8},{24,16},{9,1},{17,9},{25,17},{10,2},{18,10},{26,18},{... | collective-permute-start | bytes 2605064 | tf_op jit(solution)/shard_map/ppermute | solution.py:13
  6.7 2.0 %fusion.42 = f32[256]{0:T(256)} fusion(bf16[1,4,424,256]{3,2,1,0:T(8,128)(2,1)} %param.5), kind=kLoop, calls=%fused_computation.48 | loop fusion | flops 1302272 | bytes 869376 | tf_op jit(solution)/shard_map/reduce_sum | solution.py:30
  8.7 0.9 reshape.19
  9.6 2.2 %convert_reduce_fusion = f32[256]{0:T(256)} fusion(bf16[1,4,424,256]{3,2,1,0:T(8,128)(2,1)} %param.5), kind=kLoop, calls=%fused_computation.44 | loop fusion | flops 868096 | bytes 869376 | tf_op jit(solution)/shard_map/reduce_sum | solution.py:30
  11.7 1.4 reshape.20
  13.1 0.7 reduce_sum.73
  13.8 0.8 reduce_sum.75
  14.6 59.9 %all-reduce.2 = (f32[32]{0:T(128)S(1)}, f32[32]{0:T(128)S(1)}) all-reduce(f32[32]{0:T(128)S(1)} %reduce_sum.75, f32[32]{0:T(128)} %reduce_sum.73), channel_id=1, replica_groups=mesh['frames'=4,'rows'=8] {'frames','rows'}, use_global_device_ids=true, to_apply=%region_5.6 | all-reduce | flops 64 | bytes 512 | tf_op jit(solution)/shard_map/psum | solution.py:68
  75.8 0.7 broadcast_in_dim.19
  76.5 0.6 sub.30
  77.1 2.6 %pad_maximum_fusion = (bf16[3,1,424,256]{3,2,0,1:T(8,128)(2,1)}, bf16[3,1,424,256]{3,2,0,1:T(8,128)(2,1)}) fusion(bf16[1,4,424,256]{3,2,0,1:T(8,128)(2,1)} %bitcast.5, bf16[1,4,424,256]{3,2,0,1:T(8,128)(2,1)} %bitcast.4, bf16[1,4,424,256]{3,2,0,1:T(8,128)(2,1)} %bitcast.148), kind=kLoop, calls=%fused_computation.76 | loop fusion | flops 1302528 | bytes 3907584 | tf_op jit(solution)/shard_map/slice | solution.py:22
  79.7 2.7 %collective-permute-start.3 = (bf16[3,1,424,256]{3,2,0,1:T(8,128)(2,1)}, bf16[3,1,424,256]{3,2,0,1:T(8,128)(2,1)}, u32[]{:S(2)}, u32[]{:S(2)}) collective-permute-start(bf16[3,1,424,256]{3,2,0,1:T(8,128)(2,1)} %get-tuple-element.20), channel_id=1, source_target_pairs={{1,0},{2,1},{3,2},{4,3},{5,4},{6,5},{7,6},{9,8},{10,9},{11,10},{12... | collective-permute-start | bytes 1953800 | tf_op jit(solution)/shard_map/ppermute | solution.py:24
  82.4 1.9 %collective-permute-start.2 = (bf16[3,1,424,256]{3,2,0,1:T(8,128)(2,1)}, bf16[3,1,424,256]{3,2,0,1:T(8,128)(2,1)}, u32[]{:S(2)}, u32[]{:S(2)}) collective-permute-start(bf16[3,1,424,256]{3,2,0,1:T(8,128)(2,1)} %get-tuple-element.21), channel_id=1, source_target_pairs={{0,1},{1,2},{2,3},{3,4},{4,5},{5,6},{6,7},{8,9},{9,10},{10,11},{11... | collective-permute-start | bytes 1953800 | tf_op jit(solution)/shard_map/ppermute | solution.py:23
  84.3 1.9 %fusion.77 = (bf16[3,1,1,256,256]{4,3,2,1,0:T(8,128)(2,1)}, bf16[3,1,1,256,256]{4,3,2,1,0:T(8,128)(2,1)}, bf16[3,1,1,256,256]{4,3,2,1,0:T(8,128)(2,1)}, bf16[3,1...) fusion(bf16[3,3,3,256,256]{4,3,2,1,0:T(8,128)(2,1)S(1)} %copy-d, ...), kind=kLoop, calls=%fused_computation.95 | loop fusion | bytes 7077888 | tf_op jit(solution)/shard_map/slice | solution.py:49
  86.2 1.9 %slice.117 = bf16[3,1,1,256,256]{4,3,2,1,0:T(8,128)(2,1)} reverse(bf16[3,1,1,256,256]{4,3,2,1,0:T(8,128)(2,1)} %get-tuple-element.11), dimensions={0} | reverse | bytes 786432 | tf_op jit(solution)/shard_map/slice | solution.py:49
  88.1 1.8 %slice.111 = bf16[3,1,1,256,256]{4,3,2,1,0:T(8,128)(2,1)} reverse(bf16[3,1,1,256,256]{4,3,2,1,0:T(8,128)(2,1)} %get-tuple-element.12), dimensions={0} | reverse | bytes 786432 | tf_op jit(solution)/shard_map/slice | solution.py:49
  89.9 1.8 %slice.108 = bf16[3,1,1,256,256]{4,3,2,1,0:T(8,128)(2,1)} reverse(bf16[3,1,1,256,256]{4,3,2,1,0:T(8,128)(2,1)} %get-tuple-element.13), dimensions={0} | reverse | bytes 786432 | tf_op jit(solution)/shard_map/slice | solution.py:49
  91.8 0.8 slice.105
  92.8 0.8 slice.114
  93.6 2.4 %fusion.34 = f32[4,424,256,1]{2,1,3,0:T(8,128)S(1)} fusion(bf16[1,4,424,256]{3,2,0,1:T(8,128)(2,1)} %bitcast.5, bf16[1,4,424,256]{3,2,0,1:T(8,128)(2,1)} %bitcast.4, bf16[1,4,424,256]{3,2,0,1:T(8,128)(2,1)S(1)} %bitcast.149, bf16[3,1,1,256,256]{4,3,2,1,0:T(8,128)(2,1)} %slice.105), kind=kOutput, calls=%fused_computation.38 | convolution fusion | flops 669499392 | bytes 4734976 | tf_op jit(solution)/shard_map/myxo,mco->yxc/dot_general | solution.py:46
  96.0 4.5 %select_maximum_fusion = bf16[3,6,426,256]{3,2,0,1:T(8,128)(2,1)S(1)} fusion(bf16[3,1,424,256]{3,2,0,1:T(8,128)(2,1)} %collective-permute-done.3, bf16[3,1,424,256]{3,2,0,1:T(8,128)(2,1)} %collective-permute-done.2, bf16[1,4,424,256]{3,2,0,1:T(8,128)(2,1)} %bitcast.5, bf16[1,4,424,256]{3,2,0,1:T(8,128)(2,1)} %bitcast.4, bf16[1,4,424,256]{3,2,0,1:T(8,128)(2,1)S(1)} %bitcast.150), kind=kLoop, calls=%fused_computation.3 | loop fusion | flops 35334144 | bytes 7833600 | tf_op jit(solution)/shard_map/concatenate | solution.py:25
  100.5 1.0 fusion.24
  101.5 0.9 fusion.26
  102.5 1.0 fusion.28
  103.4 0.9 fusion.30
  104.4 1.0 fusion.32
  105.4 2.4 %fusion.14 = f32[4,424,256,1]{2,1,3,0:T(8,128)S(1)} fusion(bf16[1,4,424,256]{3,2,0,1:T(8,128)(2,1)} %bitcast.5, bf16[1,4,424,256]{3,2,0,1:T(8,128)(2,1)} %bitcast.4, bf16[1,4,424,256]{3,2,0,1:T(8,128)(2,1)S(1)} %bitcast.151, bf16[3,1,424,256]{3,2,0,1:T(8,128)(2,1)} %collective-permute-done.2, bf16[3,1,1,256,256]{4,3,2,1,0:T(8,128)(2,1)S(1)} %copy-done.12), kind=kOutput, calls=%fused_computation.18 | convolution fusion | flops 679919616 | bytes 5386240 | tf_op jit(solution)/shard_map/myxo,mco->yxc/dot_general | solution.py:46
  107.8 2.5 %fusion.6 = f32[4,424,256,1]{2,1,3,0:T(8,128)S(1)} fusion(bf16[3,1,424,256]{3,2,0,1:T(8,128)(2,1)} %collective-permute-done.3, bf16[1,4,424,256]{3,2,0,1:T(8,128)(2,1)} %bitcast.5, bf16[1,4,424,256]{3,2,0,1:T(8,128)(2,1)} %bitcast.4, bf16[1,4,424,256]{3,2,0,1:T(8,128)(2,1)S(1)} %bitcast.152, bf16[3,1,1,256,256]{4,3,2,1,0:T(8,128)(2,1)S(1)} %slice.97), kind=kOutput, calls=%fused_computation.10 | convolution fusion | flops 679919616 | bytes 5386240 | tf_op jit(solution)/shard_map/myxo,mco->yxc/dot_general | solution.py:46
  110.3 2.1 %fusion.76 = (f32[256]{0:T(256)S(1)}, f32[256]{0:T(256)S(1)}, f32[4,424,256]{2,1,0:T(8,128)S(1)}) fusion(f32[256]{0:T(256)S(1)} %copy-done.13, f32[256]{0:T(256)S(1)} %copy-done.14, bf16[1,4,424,256]{3,2,1,0:T(8,128)(2,1)S(1)} %copy-done, f32[256]{0:T(256)S(1)} %copy-done.15, f32[256]{0:T(256)S(1)} %copy-done.16, ...), kind=kOutput, calls=%fused_computation.94 | convolution fusion | flops 677748224 | bytes 19503104 | tf_op jit(solution)/shard_map/myxo,mco->yxc/dot_general | solution.py:46
  112.9 42.1 %all-reduce.1 = (f32[32]{0:T(128)S(1)}, f32[32]{0:T(128)S(1)}) all-reduce(f32[32]{0:T(128)S(1)} %reduce_sum.79, f32[32]{0:T(128)S(1)} %reduce_sum.77), channel_id=1, replica_groups=mesh['frames'=4,'rows'=8] {'frames','rows'}, use_global_device_ids=true, to_apply=%region_11.12 | all-reduce | flops 64 | bytes 512 | tf_op jit(solution)/shard_map/psum | solution.py:77
  155.3 1.3 fusion.63
  (54 shorter events, 2.2 us)
Async XLA Ops:
  0.0 77.1 %collective-permute-start.1 = (bf16[4,424,256]{2,1,0:T(8,128)(2,1)}, bf16[4,424,256]{2,1,0:T(8,128)(2,1)}, u32[]{:S(2)}, u32[]{:S(2)}) collective-permute-start(bf16[4,424,256]{2,1,0:T(8,128)(2,1)} %bitcast.146), channel_id=1, source_target_pairs={{16,0},{24,8},{17,1},{25,9},{18,2},{26,10},{19,3},{27,11},{20,4},{... | collective-permute-start | bytes 2605064 | tf_op jit(solution)/shard_map/ppermute | solution.py:13
  3.3 73.8 %collective-permute-start = (bf16[4,424,256]{2,1,0:T(8,128)(2,1)}, bf16[4,424,256]{2,1,0:T(8,128)(2,1)}, u32[]{:S(2)}, u32[]{:S(2)}) collective-permute-start(bf16[4,424,256]{2,1,0:T(8,128)(2,1)} %bitcast.147), channel_id=1, source_target_pairs={{8,0},{16,8},{24,16},{9,1},{17,9},{25,17},{10,2},{18,10},{26,18},{... | collective-permute-start | bytes 2605064 | tf_op jit(solution)/shard_map/ppermute | solution.py:13
  8.7 75.7 %copy-start.1 = (bf16[3,3,3,256,256]{4,3,2,1,0:T(8,128)(2,1)S(1)}, bf16[3,3,3,256,256]{4,3,2,1,0:T(8,128)(2,1)}, u32[]{:S(2)}) copy-start(bf16[3,3,3,256,256]{4,3,2,1,0:T(8,128)(2,1)} %param.7) | copy-start | bytes 10616836
  79.7 16.3 %collective-permute-start.3 = (bf16[3,1,424,256]{3,2,0,1:T(8,128)(2,1)}, bf16[3,1,424,256]{3,2,0,1:T(8,128)(2,1)}, u32[]{:S(2)}, u32[]{:S(2)}) collective-permute-start(bf16[3,1,424,256]{3,2,0,1:T(8,128)(2,1)} %get-tuple-element.20), channel_id=1, source_target_pairs={{1,0},{2,1},{3,2},{4,3},{5,4},{6,5},{7,6},{9,8},{10,9},{11,10},{12... | collective-permute-start | bytes 1953800 | tf_op jit(solution)/shard_map/ppermute | solution.py:24
  82.4 13.6 %collective-permute-start.2 = (bf16[3,1,424,256]{3,2,0,1:T(8,128)(2,1)}, bf16[3,1,424,256]{3,2,0,1:T(8,128)(2,1)}, u32[]{:S(2)}, u32[]{:S(2)}) collective-permute-start(bf16[3,1,424,256]{3,2,0,1:T(8,128)(2,1)} %get-tuple-element.21), channel_id=1, source_target_pairs={{0,1},{1,2},{2,3},{3,4},{4,5},{5,6},{6,7},{8,9},{9,10},{10,11},{11... | collective-permute-start | bytes 1953800 | tf_op jit(solution)/shard_map/ppermute | solution.py:23
  86.2 5.6 %copy-start.8 = (bf16[3,1,1,256,256]{4,3,2,1,0:T(8,128)(2,1)S(1)}, bf16[3,1,1,256,256]{4,3,2,1,0:T(8,128)(2,1)}, u32[]{:S(2)}) copy-start(bf16[3,1,1,256,256]{4,3,2,1,0:T(8,128)(2,1)} %get-tuple-element.14) | copy-start | bytes 1179652
  86.2 6.4 %copy-start.7 = (bf16[3,1,1,256,256]{4,3,2,1,0:T(8,128)(2,1)S(1)}, bf16[3,1,1,256,256]{4,3,2,1,0:T(8,128)(2,1)}, u32[]{:S(2)}) copy-start(bf16[3,1,1,256,256]{4,3,2,1,0:T(8,128)(2,1)} %get-tuple-element.15) | copy-start | bytes 1179652
  86.2 6.4 %copy-start.6 = (bf16[3,1,1,256,256]{4,3,2,1,0:T(8,128)(2,1)S(1)}, bf16[3,1,1,256,256]{4,3,2,1,0:T(8,128)(2,1)}, u32[]{:S(2)}) copy-start(bf16[3,1,1,256,256]{4,3,2,1,0:T(8,128)(2,1)} %get-tuple-element.16) | copy-start | bytes 1179652
  86.2 6.5 %copy-start.5 = (bf16[3,1,1,256,256]{4,3,2,1,0:T(8,128)(2,1)S(1)}, bf16[3,1,1,256,256]{4,3,2,1,0:T(8,128)(2,1)}, u32[]{:S(2)}) copy-start(bf16[3,1,1,256,256]{4,3,2,1,0:T(8,128)(2,1)} %get-tuple-element.17) | copy-start | bytes 1179652
  86.2 6.5 %copy-start.4 = (bf16[3,1,1,256,256]{4,3,2,1,0:T(8,128)(2,1)S(1)}, bf16[3,1,1,256,256]{4,3,2,1,0:T(8,128)(2,1)}, u32[]{:S(2)}) copy-start(bf16[3,1,1,256,256]{4,3,2,1,0:T(8,128)(2,1)} %get-tuple-element.18) | copy-start | bytes 1179652
  88.1 4.6 %copy-start.3 = (bf16[3,1,1,256,256]{4,3,2,1,0:T(8,128)(2,1)S(1)}, bf16[3,1,1,256,256]{4,3,2,1,0:T(8,128)(2,1)}, u32[]{:S(2)}) copy-start(bf16[3,1,1,256,256]{4,3,2,1,0:T(8,128)(2,1)} %get-tuple-element.19) | copy-start | bytes 1179652
  89.9 3.6 %copy-start.2 = (bf16[1,4,424,256]{3,2,1,0:T(8,128)(2,1)S(1)}, bf16[1,4,424,256]{3,2,1,0:T(8,128)(2,1)}, u32[]{:S(2)}) copy-start(bf16[1,4,424,256]{3,2,1,0:T(8,128)(2,1)} %param.6) | copy-start | bytes 2605060
  96.0 4.5 %copy-start.10 = (bf16[3,1,1,256,256]{4,3,2,1,0:T(8,128)(2,1)S(1)}, bf16[3,1,1,256,256]{4,3,2,1,0:T(8,128)(2,1)}, u32[]{:S(2)}) copy-start(bf16[3,1,1,256,256]{4,3,2,1,0:T(8,128)(2,1)} %slice.111) | copy-start | bytes 1179652
  100.5 1.0 copy-start.11
  104.4 1.0 copy-start.12
  107.7 2.5 %copy-start = (bf16[1,4,424,256]{3,2,1,0:T(8,128)(2,1)S(1)}, bf16[1,4,424,256]{3,2,1,0:T(8,128)(2,1)}, u32[]{:S(2)}) copy-start(bf16[1,4,424,256]{3,2,1,0:T(8,128)(2,1)} %param.5) | copy-start | bytes 2605060
  107.8 2.5 %copy-start.9 = (bf16[3,1,1,256,256]{4,3,2,1,0:T(8,128)(2,1)S(1)}, bf16[3,1,1,256,256]{4,3,2,1,0:T(8,128)(2,1)}, u32[]{:S(2)}) copy-start(bf16[3,1,1,256,256]{4,3,2,1,0:T(8,128)(2,1)} %slice.117) | copy-start | bytes 1179652
  107.8 2.5 %copy-start.13 = (f32[256]{0:T(256)S(1)}, f32[256]{0:T(256)}, u32[]{:S(2)}) copy-start(f32[256]{0:T(256)} %mul.60) | copy-start | bytes 3076
  107.8 2.5 %copy-start.14 = (f32[256]{0:T(256)S(1)}, f32[256]{0:T(256)}, u32[]{:S(2)}) copy-start(f32[256]{0:T(256)} %sub.30) | copy-start | bytes 3076
  107.8 2.5 %copy-start.15 = (f32[256]{0:T(256)S(1)}, f32[256]{0:T(256)}, u32[]{:S(2)}) copy-start(f32[256]{0:T(256)} %param.9) | copy-start | bytes 3076
  107.8 2.5 %copy-start.16 = (f32[256]{0:T(256)S(1)}, f32[256]{0:T(256)}, u32[]{:S(2)}) copy-start(f32[256]{0:T(256)} %param.8) | copy-start | bytes 3076
where the time goes:
time: 157 us
  blocking collectives  102 us (65%)
  other arithmetic  14.9 us (9%)
  matrix products  14.1 us (9%)
  local copies, waits for them, and re-layouts  14 us (9%)
  starting transfers between devices  11.3 us (7%)
    psum x1, blocking collectives, shards(): lax.psum((group_sum(values), group_sum(values * values)), ('frames', 'row...  59.9 us
    psum x1, blocking collectives, shards(): lax.psum((group_sum(norm_grad), group_sum(norm_grad * normed)), ('frames'...  42.1 us
    dot_general x9, matrix products, transpose_conv(): jnp.einsum('myxo,mco->yxc', window, flipped[:, row_tap, col_tap], preferr...  14.1 us
    slice x10, local copies, waits for them, and re-layouts, transpose_conv(): flipped[:, row_tap, col_tap]  9.11 us
    ppermute x2, starting transfers between devices, from_behind(): return lax.ppermute(value, axis, pairs)  6.69 us
    concatenate x1, other arithmetic, padded_2(): value = jnp.concatenate([before, value, after], axis=dim)  4.5 us
    reduce_sum x2, other arithmetic, group_sum(): per_chan = jnp.sum(values, axis=(0, 1))  4.14 us
  transfers between devices with their start and end apart: 4, of which 0 were waited for; matrix products, arithmetic and copies ran while one was open for 14% of the time, Pallas kernels for 0%

commit v1 on v0

--- a/solution.py
+++ b/solution.py
@@ -5,6 +5,11 @@
 
 GROUPS = 32
 EPS = 1e-06
+
+
+def by_each_axis(value_2, axis_one, axis_two):
+    partial = lax.psum(value_2, axis_one)
+    return lax.psum(partial, axis_two)
 
 
 def from_behind(value, axis, by):
@@ -74,8 +79,8 @@
     preact = normed * norm_gain + norm_bias
     logistic = jax.nn.sigmoid(preact)
     norm_grad = act_grad * logistic * (1.0 + preact * (1.0 - logistic)) * norm_gain
-    grad_total, grad_cross = lax.psum(
-        (group_sum(norm_grad), group_sum(norm_grad * normed)), ("frames", "rows")
+    grad_total, grad_cross = by_each_axis(
+        (group_sum(norm_grad), group_sum(norm_grad * normed)), "rows", "frames"
     )
     grad_total = grad_total / cells_per
     grad_cross = grad_cross / cells_per

time: 157 us -> 143 us (0.911)
  the two profiles are of different devices: /device:TPU:14 before, /device:TPU:0 now
where the time goes in v1:
time: 143 us; the launch traced here: 142 us
  blocking collectives  91.2 us (64%)
  other arithmetic  14.9 us (10%)
  matrix products  14.1 us (10%)
  local copies, waits for them, and re-layouts  14 us (10%)
  starting transfers between devices  7.73 us (5%)
    psum x1, blocking collectives, shards(): lax.psum((group_sum(values), group_sum(values * values)), ('frames', 'row...  67.4 us
    psum x1, blocking collectives, by_each_axis(): partial = lax.psum(value_2, axis_one)  14.1 us
    dot_general x9, matrix products, transpose_conv(): jnp.einsum('myxo,mco->yxc', window, flipped[:, row_tap, col_tap], preferr...  14.1 us
    psum x1, blocking collectives, by_each_axis(): return lax.psum(partial, axis_two)  9.74 us
    slice x10, local copies, waits for them, and re-layouts, transpose_conv(): flipped[:, row_tap, col_tap]  9.11 us
    concatenate x1, other arithmetic, padded_2(): value = jnp.concatenate([before, value, after], axis=dim)  4.5 us
    reduce_sum x2, other arithmetic, group_sum(): per_chan = jnp.sum(values, axis=(0, 1))  4.14 us
    ppermute x1, starting transfers between devices, padded_2(): before = lax.ppermute(last, axis, up)  3.87 us
  transfers between devices with their start and end apart: 4, of which 0 were waited for; matrix products, arithmetic and copies ran while one was open for 15% of the time, Pallas kernels for 0%

profile of v1, /device:TPU:0, one launch (start us, length us, event | category | flops | bytes accessed | tf_op | source)
XLA Modules:
  0.0 142.3 jit_solution(3402151632776045116)
XLA Ops:
  0.0 1.3 collective-permute-start.1
  1.3 1.3 collective-permute-start
  2.6 2.0 %fusion.42 = f32[256]{0:T(256)} fusion(bf16[1,4,424,256]{3,2,1,0:T(8,128)(2,1)} %param.5), kind=kLoop, calls=%fused_computation.48 | loop fusion | flops 1302272 | bytes 869376 | tf_op jit(solution)/shard_map/reduce_sum | solution.py:35
  4.6 0.9 reshape.19
  5.5 2.2 %convert_reduce_fusion = f32[256]{0:T(256)} fusion(bf16[1,4,424,256]{3,2,1,0:T(8,128)(2,1)} %param.5), kind=kLoop, calls=%fused_computation.44 | loop fusion | flops 868096 | bytes 869376 | tf_op jit(solution)/shard_map/reduce_sum | solution.py:35
  7.6 1.4 reshape.20
  9.0 0.7 reduce_sum.73
  9.7 0.8 reduce_sum.75
  10.5 67.4 %all-reduce.1 = (f32[32]{0:T(128)S(1)}, f32[32]{0:T(128)S(1)}) all-reduce(f32[32]{0:T(128)S(1)} %reduce_sum.75, f32[32]{0:T(128)} %reduce_sum.73), channel_id=1, replica_groups=mesh['frames'=4,'rows'=8] {'frames','rows'}, use_global_device_ids=true, to_apply=%region_5.6 | all-reduce | flops 64 | bytes 512 | tf_op jit(solution)/shard_map/psum | solution.py:73
  79.1 0.7 broadcast_in_dim.19
  80.5 2.6 %pad_maximum_fusion = (bf16[3,1,424,256]{3,2,0,1:T(8,128)(2,1)}, bf16[3,1,424,256]{3,2,0,1:T(8,128)(2,1)}) fusion(bf16[1,4,424,256]{3,2,0,1:T(8,128)(2,1)} %bitcast.5, bf16[1,4,424,256]{3,2,0,1:T(8,128)(2,1)} %bitcast.4, bf16[1,4,424,256]{3,2,0,1:T(8,128)(2,1)} %bitcast.148), kind=kLoop, calls=%fused_computation.76 | loop fusion | flops 1302528 | bytes 3907584 | tf_op jit(solution)/shard_map/slice | solution.py:27
  83.1 1.3 collective-permute-start.3
  84.4 3.9 %collective-permute-start.2 = (bf16[3,1,424,256]{3,2,0,1:T(8,128)(2,1)}, bf16[3,1,424,256]{3,2,0,1:T(8,128)(2,1)}, u32[]{:S(2)}, u32[]{:S(2)}) collective-permute-start(bf16[3,1,424,256]{3,2,0,1:T(8,128)(2,1)} %get-tuple-element.23), channel_id=1, source_target_pairs={{0,1},{1,2},{2,3},{3,4},{4,5},{5,6},{6,7},{8,9},{9,10},{10,11},{11... | collective-permute-start | bytes 1953800 | tf_op jit(solution)/shard_map/ppermute | solution.py:28
  88.2 1.9 %fusion.77 = (bf16[3,1,1,256,256]{4,3,2,1,0:T(8,128)(2,1)}, bf16[3,1,1,256,256]{4,3,2,1,0:T(8,128)(2,1)}, bf16[3,1,1,256,256]{4,3,2,1,0:T(8,128)(2,1)}, bf16[3,1...) fusion(bf16[3,3,3,256,256]{4,3,2,1,0:T(8,128)(2,1)S(1)} %copy-d, ...), kind=kLoop, calls=%fused_computation.95 | loop fusion | bytes 7077888 | tf_op jit(solution)/shard_map/slice | solution.py:54
  90.1 1.9 %slice.117 = bf16[3,1,1,256,256]{4,3,2,1,0:T(8,128)(2,1)} reverse(bf16[3,1,1,256,256]{4,3,2,1,0:T(8,128)(2,1)} %get-tuple-element.13), dimensions={0} | reverse | bytes 786432 | tf_op jit(solution)/shard_map/slice | solution.py:54
  92.0 1.8 %slice.111 = bf16[3,1,1,256,256]{4,3,2,1,0:T(8,128)(2,1)} reverse(bf16[3,1,1,256,256]{4,3,2,1,0:T(8,128)(2,1)} %get-tuple-element.14), dimensions={0} | reverse | bytes 786432 | tf_op jit(solution)/shard_map/slice | solution.py:54
  93.8 1.8 %slice.108 = bf16[3,1,1,256,256]{4,3,2,1,0:T(8,128)(2,1)} reverse(bf16[3,1,1,256,256]{4,3,2,1,0:T(8,128)(2,1)} %get-tuple-element.15), dimensions={0} | reverse | bytes 786432 | tf_op jit(solution)/shard_map/slice | solution.py:54
  95.7 0.8 slice.105
  96.7 0.8 slice.114
  97.4 2.4 %fusion.34 = f32[4,424,256,1]{2,1,3,0:T(8,128)S(1)} fusion(bf16[1,4,424,256]{3,2,0,1:T(8,128)(2,1)} %bitcast.5, bf16[1,4,424,256]{3,2,0,1:T(8,128)(2,1)} %bitcast.4, bf16[1,4,424,256]{3,2,0,1:T(8,128)(2,1)S(1)} %bitcast.149, bf16[3,1,1,256,256]{4,3,2,1,0:T(8,128)(2,1)} %slice.105), kind=kOutput, calls=%fused_computation.38 | convolution fusion | flops 669499392 | bytes 4734976 | tf_op jit(solution)/shard_map/myxo,mco->yxc/dot_general | solution.py:51
  99.9 4.5 %select_maximum_fusion = bf16[3,6,426,256]{3,2,0,1:T(8,128)(2,1)S(1)} fusion(bf16[3,1,424,256]{3,2,0,1:T(8,128)(2,1)} %collective-permute-done.3, bf16[3,1,424,256]{3,2,0,1:T(8,128)(2,1)} %collective-permute-done.2, bf16[1,4,424,256]{3,2,0,1:T(8,128)(2,1)} %bitcast.5, bf16[1,4,424,256]{3,2,0,1:T(8,128)(2,1)} %bitcast.4, bf16[1,4,424,256]{3,2,0,1:T(8,128)(2,1)S(1)} %bitcast.150), kind=kLoop, calls=%fused_computation.3 | loop fusion | flops 35334144 | bytes 7833600 | tf_op jit(solution)/shard_map/concatenate | solution.py:30
  104.4 1.0 fusion.24
  105.4 0.9 fusion.26
  106.4 1.0 fusion.28
  107.3 0.9 fusion.30
  108.3 1.0 fusion.32
  109.3 2.4 %fusion.14 = f32[4,424,256,1]{2,1,3,0:T(8,128)S(1)} fusion(bf16[1,4,424,256]{3,2,0,1:T(8,128)(2,1)} %bitcast.5, bf16[1,4,424,256]{3,2,0,1:T(8,128)(2,1)} %bitcast.4, bf16[1,4,424,256]{3,2,0,1:T(8,128)(2,1)S(1)} %bitcast.151, bf16[3,1,424,256]{3,2,0,1:T(8,128)(2,1)} %collective-permute-done.2, bf16[3,1,1,256,256]{4,3,2,1,0:T(8,128)(2,1)S(1)} %copy-done.12), kind=kOutput, calls=%fused_computation.18 | convolution fusion | flops 679919616 | bytes 5386240 | tf_op jit(solution)/shard_map/myxo,mco->yxc/dot_general | solution.py:51
  111.7 2.5 %fusion.6 = f32[4,424,256,1]{2,1,3,0:T(8,128)S(1)} fusion(bf16[3,1,424,256]{3,2,0,1:T(8,128)(2,1)} %collective-permute-done.3, bf16[1,4,424,256]{3,2,0,1:T(8,128)(2,1)} %bitcast.5, bf16[1,4,424,256]{3,2,0,1:T(8,128)(2,1)} %bitcast.4, bf16[1,4,424,256]{3,2,0,1:T(8,128)(2,1)S(1)} %bitcast.152, bf16[3,1,1,256,256]{4,3,2,1,0:T(8,128)(2,1)S(1)} %slice.97), kind=kOutput, calls=%fused_computation.10 | convolution fusion | flops 679919616 | bytes 5386240 | tf_op jit(solution)/shard_map/myxo,mco->yxc/dot_general | solution.py:51
  114.2 2.1 %fusion.76 = (f32[256]{0:T(256)S(1)}, f32[256]{0:T(256)S(1)}, f32[4,424,256]{2,1,0:T(8,128)S(1)}) fusion(f32[256]{0:T(256)S(1)} %copy-done.13, f32[256]{0:T(256)S(1)} %copy-done.14, bf16[1,4,424,256]{3,2,1,0:T(8,128)(2,1)S(1)} %copy-done, f32[256]{0:T(256)S(1)} %copy-done.15, f32[256]{0:T(256)S(1)} %copy-done.16, ...), kind=kOutput, calls=%fused_computation.94 | convolution fusion | flops 677748224 | bytes 19503104 | tf_op jit(solution)/shard_map/myxo,mco->yxc/dot_general | solution.py:51
  116.7 14.1 %all-reduce.2 = (f32[32]{0:T(128)S(1)}, f32[32]{0:T(128)S(1)}) all-reduce(f32[32]{0:T(128)S(1)} %reduce_sum.79, f32[32]{0:T(128)S(1)} %reduce_sum.77), channel_id=1, replica_groups=mesh['frames'=4,'rows'=8] {'rows'}, use_global_device_ids=true, to_apply=%region_12.13 | all-reduce | flops 64 | bytes 512 | tf_op jit(solution)/shard_map/psum | solution.py:11
  130.9 9.7 %all-reduce.3 = (f32[32]{0:T(128)S(1)}, f32[32]{0:T(128)S(1)}) all-reduce(f32[32]{0:T(128)S(1)} %get-tuple-element.9, f32[32]{0:T(128)S(1)} %get-tuple-element.10), channel_id=1, replica_groups=mesh['frames'=4,'rows'=8] {'frames'}, use_global_device_ids=true, to_apply=%region_13.14 | all-reduce | flops 64 | bytes 512 | tf_op jit(solution)/shard_map/psum | solution.py:12
  140.9 1.3 fusion.63
  (55 shorter events, 2.8 us)
Async XLA Ops:
  0.0 80.5 %collective-permute-start.1 = (bf16[4,424,256]{2,1,0:T(8,128)(2,1)}, bf16[4,424,256]{2,1,0:T(8,128)(2,1)}, u32[]{:S(2)}, u32[]{:S(2)}) collective-permute-start(bf16[4,424,256]{2,1,0:T(8,128)(2,1)} %bitcast.146), channel_id=1, source_target_pairs={{16,0},{24,8},{17,1},{25,9},{18,2},{26,10},{19,3},{27,11},{20,4},{... | collective-permute-start | bytes 2605064 | tf_op jit(solution)/shard_map/ppermute | solution.py:18
  1.3 79.2 %collective-permute-start = (bf16[4,424,256]{2,1,0:T(8,128)(2,1)}, bf16[4,424,256]{2,1,0:T(8,128)(2,1)}, u32[]{:S(2)}, u32[]{:S(2)}) collective-permute-start(bf16[4,424,256]{2,1,0:T(8,128)(2,1)} %bitcast.147), channel_id=1, source_target_pairs={{8,0},{16,8},{24,16},{9,1},{17,9},{25,17},{10,2},{18,10},{26,18},{... | collective-permute-start | bytes 2605064 | tf_op jit(solution)/shard_map/ppermute | solution.py:18
  4.6 83.7 %copy-start.1 = (bf16[3,3,3,256,256]{4,3,2,1,0:T(8,128)(2,1)S(1)}, bf16[3,3,3,256,256]{4,3,2,1,0:T(8,128)(2,1)}, u32[]{:S(2)}) copy-start(bf16[3,3,3,256,256]{4,3,2,1,0:T(8,128)(2,1)} %param.7) | copy-start | bytes 10616836
  83.1 16.8 %collective-permute-start.3 = (bf16[3,1,424,256]{3,2,0,1:T(8,128)(2,1)}, bf16[3,1,424,256]{3,2,0,1:T(8,128)(2,1)}, u32[]{:S(2)}, u32[]{:S(2)}) collective-permute-start(bf16[3,1,424,256]{3,2,0,1:T(8,128)(2,1)} %get-tuple-element.22), channel_id=1, source_target_pairs={{1,0},{2,1},{3,2},{4,3},{5,4},{6,5},{7,6},{9,8},{10,9},{11,10},{12... | collective-permute-start | bytes 1953800 | tf_op jit(solution)/shard_map/ppermute | solution.py:29
  84.4 15.5 %collective-permute-start.2 = (bf16[3,1,424,256]{3,2,0,1:T(8,128)(2,1)}, bf16[3,1,424,256]{3,2,0,1:T(8,128)(2,1)}, u32[]{:S(2)}, u32[]{:S(2)}) collective-permute-start(bf16[3,1,424,256]{3,2,0,1:T(8,128)(2,1)} %get-tuple-element.23), channel_id=1, source_target_pairs={{0,1},{1,2},{2,3},{3,4},{4,5},{5,6},{6,7},{8,9},{9,10},{10,11},{11... | collective-permute-start | bytes 1953800 | tf_op jit(solution)/shard_map/ppermute | solution.py:28
  90.1 5.6 %copy-start.8 = (bf16[3,1,1,256,256]{4,3,2,1,0:T(8,128)(2,1)S(1)}, bf16[3,1,1,256,256]{4,3,2,1,0:T(8,128)(2,1)}, u32[]{:S(2)}) copy-start(bf16[3,1,1,256,256]{4,3,2,1,0:T(8,128)(2,1)} %get-tuple-element.16) | copy-start | bytes 1179652
  90.1 6.4 %copy-start.7 = (bf16[3,1,1,256,256]{4,3,2,1,0:T(8,128)(2,1)S(1)}, bf16[3,1,1,256,256]{4,3,2,1,0:T(8,128)(2,1)}, u32[]{:S(2)}) copy-start(bf16[3,1,1,256,256]{4,3,2,1,0:T(8,128)(2,1)} %get-tuple-element.17) | copy-start | bytes 1179652
  90.1 6.4 %copy-start.6 = (bf16[3,1,1,256,256]{4,3,2,1,0:T(8,128)(2,1)S(1)}, bf16[3,1,1,256,256]{4,3,2,1,0:T(8,128)(2,1)}, u32[]{:S(2)}) copy-start(bf16[3,1,1,256,256]{4,3,2,1,0:T(8,128)(2,1)} %get-tuple-element.18) | copy-start | bytes 1179652
  90.1 6.5 %copy-start.5 = (bf16[3,1,1,256,256]{4,3,2,1,0:T(8,128)(2,1)S(1)}, bf16[3,1,1,256,256]{4,3,2,1,0:T(8,128)(2,1)}, u32[]{:S(2)}) copy-start(bf16[3,1,1,256,256]{4,3,2,1,0:T(8,128)(2,1)} %get-tuple-element.19) | copy-start | bytes 1179652
  90.1 6.5 %copy-start.4 = (bf16[3,1,1,256,256]{4,3,2,1,0:T(8,128)(2,1)S(1)}, bf16[3,1,1,256,256]{4,3,2,1,0:T(8,128)(2,1)}, u32[]{:S(2)}) copy-start(bf16[3,1,1,256,256]{4,3,2,1,0:T(8,128)(2,1)} %get-tuple-element.20) | copy-start | bytes 1179652
  92.0 4.6 %copy-start.3 = (bf16[3,1,1,256,256]{4,3,2,1,0:T(8,128)(2,1)S(1)}, bf16[3,1,1,256,256]{4,3,2,1,0:T(8,128)(2,1)}, u32[]{:S(2)}) copy-start(bf16[3,1,1,256,256]{4,3,2,1,0:T(8,128)(2,1)} %get-tuple-element.21) | copy-start | bytes 1179652
  93.8 3.6 %copy-start.2 = (bf16[1,4,424,256]{3,2,1,0:T(8,128)(2,1)S(1)}, bf16[1,4,424,256]{3,2,1,0:T(8,128)(2,1)}, u32[]{:S(2)}) copy-start(bf16[1,4,424,256]{3,2,1,0:T(8,128)(2,1)} %param.6) | copy-start | bytes 2605060
  99.9 4.5 %copy-start.10 = (bf16[3,1,1,256,256]{4,3,2,1,0:T(8,128)(2,1)S(1)}, bf16[3,1,1,256,256]{4,3,2,1,0:T(8,128)(2,1)}, u32[]{:S(2)}) copy-start(bf16[3,1,1,256,256]{4,3,2,1,0:T(8,128)(2,1)} %slice.111) | copy-start | bytes 1179652
  104.4 1.0 copy-start.11
  108.3 1.0 copy-start.12
  111.6 2.5 %copy-start = (bf16[1,4,424,256]{3,2,1,0:T(8,128)(2,1)S(1)}, bf16[1,4,424,256]{3,2,1,0:T(8,128)(2,1)}, u32[]{:S(2)}) copy-start(bf16[1,4,424,256]{3,2,1,0:T(8,128)(2,1)} %param.5) | copy-start | bytes 2605060
  111.6 2.5 %copy-start.9 = (bf16[3,1,1,256,256]{4,3,2,1,0:T(8,128)(2,1)S(1)}, bf16[3,1,1,256,256]{4,3,2,1,0:T(8,128)(2,1)}, u32[]{:S(2)}) copy-start(bf16[3,1,1,256,256]{4,3,2,1,0:T(8,128)(2,1)} %slice.117) | copy-start | bytes 1179652
  111.7 2.5 %copy-start.13 = (f32[256]{0:T(256)S(1)}, f32[256]{0:T(256)}, u32[]{:S(2)}) copy-start(f32[256]{0:T(256)} %mul.60) | copy-start | bytes 3076
  111.7 2.5 %copy-start.14 = (f32[256]{0:T(256)S(1)}, f32[256]{0:T(256)}, u32[]{:S(2)}) copy-start(f32[256]{0:T(256)} %sub.30) | copy-start | bytes 3076
  111.7 2.5 %copy-start.15 = (f32[256]{0:T(256)S(1)}, f32[256]{0:T(256)}, u32[]{:S(2)}) copy-start(f32[256]{0:T(256)} %param.9) | copy-start | bytes 3076
  111.7 2.5 %copy-start.16 = (f32[256]{0:T(256)S(1)}, f32[256]{0:T(256)}, u32[]{:S(2)}) copy-start(f32[256]{0:T(256)} %param.8) | copy-start | bytes 3076
